TPU v7x, 128 devices: a whole 4x4x4 slice. The times are simulated.
128 devices in a mesh: mod: 8 (over z, core), row: 16 (over x, y).
Axes of the slice: x: 4, y: 4, z: 4, core: 2. Of those that a mesh axis runs over, the one named last changes fastest.
Arguments:
- activations: bfloat16 [8, 16384, 4096], P('mod', 'row'), may hold values from -6 to 6
- out_grads: bfloat16 [8, 16384, 4096], P('mod', 'row'), may hold values from -0.3125 to 0.3125
- in_projection: bfloat16 [8, 64, 4096], P('mod'), may hold values from -0.09375 to 0.09375
- out_projection: bfloat16 [8, 64, 4096], P('mod'), may hold values from -0.09375 to 0.09375
- inv_curvature: bfloat16 [8, 4096, 4096], P('mod', 'row'), as said below
- store_grads: bfloat16 [8, 12288, 4096], P('mod', 'row'), may hold values from -0.03125 to 0.03125
- lengths: int32 [64], replicated, may hold values from 64 to 128, as said below
- owners: int32 [64], replicated, may hold values from 0 to 15, as said below
Outputs:
- scores: float32 [64, 12288], P('mod', 'row')
Inputs may be any that keep to these rules, and one draw needn't show every extreme that they name: `owners`: at most 8 query examples have the same owner, and some owner has exactly 8. `lengths`: the examples of one owner hold at most 1024 tokens together, and some owner holds exactly 1024. `inv_curvature`: each module's matrix is symmetric.
All inputs are finite; a program needn't handle non-finite values.
Results may differ from a plain program's by a relative error of at most 0.0041.
Values may be sent and summed in bfloat16 or wider, within the bound.
A program may use at most 128 MiB of HBM per device.

v0:
```python
import jax
import jax.numpy as jnp
from jax import lax
from jax.sharding import PartitionSpec as P

exact_mode = lax.Precision.HIGHEST


def laid_out(pieces, dim):
    lengths = list(pieces.shape[1:])
    lengths[dim] *= pieces.shape[0]
    return jnp.moveaxis(pieces, 0, dim).reshape(lengths)


def sent_to_all(array, axis):
    peers = lax.axis_size(axis)
    return lax.all_to_all(
        jnp.broadcast_to(array[None], (peers, *array.shape)), axis, 0, 0, tiled=True
    )


def gathered_copies(array, axis, dim):
    return laid_out(sent_to_all(array, axis), dim)


def cut_along(array, dim, peers):
    lengths = array.shape
    pieces = array.reshape(*lengths[:dim], peers, lengths[dim] // peers, *lengths[dim + 1 :])
    return jnp.moveaxis(pieces, dim, 0)


def sent_and_summed(array, axis, dim):
    pieces = cut_along(array, dim, lax.axis_size(axis))
    arrived = lax.all_to_all(pieces, axis, split_axis=0, concat_axis=0, tiled=True)
    return arrived.sum(axis=0)


def contract_last(left, right):
    return lax.dot_general(
        left, right, (((1,), (1,)), ((), ())), preferred_element_type=jnp.float32
    )


def on_device(
    activations,
    out_grads,
    in_projection,
    out_projection,
    inv_curvature,
    store_grads,
    lengths,
    owners,
):
    row_id = lax.axis_index("row")
    row_count = lax.axis_size("row")
    queries = lengths.shape[0]
    tok_rows = activations.shape[1]
    rank = in_projection.shape[1]
    width = rank * rank
    capacity = 2 * queries // row_count
    examples = jnp.arange(queries, dtype=jnp.int32)
    earlier = (owners[:, None] == owners[None, :]) & (examples[None, :] < examples[:, None])
    offsets = jnp.sum(jnp.where(earlier, lengths[None, :], 0), axis=1)
    slot_rank = jnp.sum(earlier.astype(jnp.int32), axis=1)
    owned_here = owners == row_id
    slot_ids = jnp.arange(capacity, dtype=jnp.int32)
    chosen = owned_here[None, :] & (slot_rank[None, :] == slot_ids[:, None])
    slot_start = jnp.sum(jnp.where(chosen, offsets[None, :], 0), axis=1)
    slot_length = jnp.sum(jnp.where(chosen, lengths[None, :], 0), axis=1)
    positions = jnp.arange(tok_rows, dtype=jnp.int32)
    slot_member = (
        (positions[None, :] >= slot_start[:, None])
        & (positions[None, :] < (slot_start + slot_length)[:, None])
    ).astype(jnp.float32)
    in_feat = contract_last(activations[0], in_projection[0])
    out_feat = contract_last(out_grads[0], out_projection[0])
    weighted = slot_member[:, None, :] * out_feat.T[None, :, :]
    per_slot = jnp.dot(
        weighted.reshape(capacity * rank, tok_rows), in_feat, precision=exact_mode
    ).reshape(capacity, width)
    store_rows = store_grads[0]
    curvature_rows = inv_curvature[0]
    all_slots = jnp.arange(row_count * capacity, dtype=jnp.int32)
    placer = (owners * capacity + slot_rank)[:, None] == all_slots[None, :]
    gathered = gathered_copies(per_slot.astype(jnp.bfloat16), "row", 0)
    whole = jnp.dot(
        placer.astype(jnp.bfloat16), gathered, preferred_element_type=jnp.float32
    ).astype(jnp.bfloat16)
    column_part = contract_last(whole, curvature_rows).astype(jnp.bfloat16)
    scores = contract_last(gathered_copies(column_part, "row", 1), store_rows)
    total = sent_and_summed(scores, "mod", 0)
    return total


def solution(mesh):
    return jax.shard_map(
        on_device,
        mesh=mesh,
        in_specs=(
            P("mod", "row", None),
            P("mod", "row", None),
            P("mod", None, None),
            P("mod", None, None),
            P("mod", "row", None),
            P("mod", "row", None),
            P(),
            P(),
        ),
        out_specs=P("mod", "row"),
        check_vma=False,
    )
```

profile of v0, /device:TPU:1, one launch (start us, length us, event | category | flops | bytes accessed | tf_op | source)
XLA Modules:
  0.0 73.7 jit_solution(17440816999171933494)
XLA Ops:
  0.0 1.0 %convert_reduce_fusion = (s32[64]{0:T(128)S(1)}, s32[64]{0:T(128)S(1)}) fusion(s32[64]{0:T(128)} %param.15, s32[64]{0:T(128)} %param.14), kind=kLoop, calls=%fused_computation.19 | loop fusion | flops 28544 | bytes 1024 | tf_op jit(solution)/shard_map/reduce_sum | solution.py:64
  1.0 1.3 %broadcast_compare_fusion = pred[64]{0:T(512)(128)(4,1)S(1)} fusion(s32[64]{0:T(128)} %param.15, s32[]{:T(128)S(6)} %axis_index.12), kind=kLoop, calls=%fused_computation.30 | loop fusion | flops 64 | bytes 324 | tf_op jit(solution)/shard_map/eq | solution.py:65
  2.3 1.1 %select_reduce_fusion.1 = (s32[8]{0:T(128)S(1)}, s32[8]{0:T(128)S(1)}) fusion(s32[64]{0:T(128)} %param.14, s32[64]{0:T(128)S(1)} %get-tuple-element.7, pred[64]{0:T(512)(128)(4,1)S(1)} %broadcast_compare_fusion, s32[64]{0:T(128)S(1)} %get-tuple-element.8), kind=kLoop, calls=%fused_computation.25 | loop fusion | flops 3056 | bytes 896 | tf_op jit(solution)/shard_map/reduce_sum | solution.py:69
  3.4 0.1 fusion.17
  3.5 6.2 %fusion.2 = f32[64,1024]{1,0:T(8,128)S(1)} fusion(bf16[1,1024,4096]{2,1,0:T(8,128)(2,1)} %param.9, bf16[1,64,4096]{2,1,0:T(8,128)(2,1)} %param.11), kind=kOutput, calls=%fused_computation.2 | convolution fusion | flops 536870912 | bytes 9175040 | tf_op jit(solution)/shard_map/dot_general | solution.py:39
  9.7 0.3 broadcast_multiply_fusion
  10.0 0.0 copy-done.2
  10.0 0.0 copy-done.1
  10.0 0.0 copy-start.3
  10.0 2.7 %fusion = f32[1024,64]{0,1:T(8,128)S(1)} fusion(bf16[1,1024,4096]{2,1,0:T(8,128)(2,1)S(1)} %copy-done.1, bf16[1,64,4096]{2,1,0:T(8,128)(2,1)S(1)} %copy-done.2), kind=kOutput, calls=%fused_computation | convolution fusion | flops 536870912 | bytes 9175040 | tf_op jit(solution)/shard_map/dot_general | solution.py:39
  12.7 2.2 %convolution_convert_fusion.1 = bf16[512,64]{0,1:T(8,128)(2,1)S(1)} fusion(f32[512,1024]{1,0:T(8,128)S(1)} %bitcast.30, f32[1024,64]{0,1:T(8,128)S(1)} %fusion), kind=kOutput, calls=%fused_computation.9 | convolution fusion | flops 402685952 | bytes 2424832 | tf_op jit(solution)/shard_map/dot_general | solution.py:78
  14.8 0.1 copy.12
  15.0 0.2 convert_element_type.30
  15.2 1.1 %broadcast_in_dim.39 = bf16[16,8,4096]{2,1,0:T(8,128)(2,1)} broadcast(bf16[8,4096]{1,0:T(8,128)(2,1)S(1)} %convert_element_type.30), dimensions={1,2} | broadcast | bytes 1114112 | tf_op jit(solution)/shard_map/broadcast_in_dim | solution.py:18
  16.3 7.6 %all-to-all-start = ((bf16[16,8,4096]{2,1,0:T(8,128)(2,1)}), bf16[16,8,4096]{2,1,0:T(8,128)(2,1)S(1)}, u32[]{:S(2)}, u32[]{:S(2)}) async-start(bf16[16,8,4096]{2,1,0:T(8,128)(2,1)} %broadcast_in_dim.39), calls=%async_computation | async-start | bytes 2097152 | tf_op jit(solution)/shard_map/all_to_all | solution.py:17
  23.9 15.6 %all-to-all-done = bf16[16,8,4096]{2,1,0:T(8,128)(2,1)S(1)} async-done(((bf16[16,8,4096]{2,1,0:T(8,128)(2,1)}), bf16[16,8,4096]{2,1,0:T(8,128)(2,1)S(1)}, u32[]{:S(2)}, u32[]{:S(2)}) %all-to-all-start) | async-done | bytes 1048608 | tf_op jit(solution)/shard_map/all_to_all | solution.py:17
  39.5 1.0 %fusion.8 = bf16[64,256]{1,0:T(8,128)(2,1)S(1)} fusion(bf16[1,256,4096]{2,1,0:T(8,128)(2,1)S(1)} %copy-done, bf16[16,8,4096]{2,1,0:T(8,128)(2,1)S(1)} %all-to-all-done, s32[64]{0:T(128)S(1)} %multiply_add_fusion), kind=kOutput, calls=%fused_computation.10 | convolution fusion | flops 201613312 | bytes 3178752 | tf_op jit(solution)/shard_map/dot_general | solution.py:39
  40.5 0.1 broadcast_in_dim.40
  40.6 12.9 %all_to_all.15 = bf16[16,64,256]{2,1,0:T(8,128)(2,1)S(1)} all-to-all(bf16[16,64,256]{2,1,0:T(8,128)(2,1)S(1)} %broadcast_in_dim.40), channel_id=1, replica_groups=mesh['mod'=8,'row'=16] {'row'}, dimensions={0} | all-to-all | bytes 1048576 | tf_op jit(solution)/shard_map/all_to_all | solution.py:17
  53.5 0.3 copy.13
  53.8 0.2 dot_general.25
  54.0 4.8 %fusion.4 = f32[8,8,768]{2,1,0:T(8,128)S(1)} fusion(bf16[8,8,4096]{2,1,0:T(8,128)(2,1)S(1)} %dot_general.25, bf16[1,768,4096]{2,1,0:T(8,128)(2,1)} %param.13), kind=kOutput, calls=%fused_computation.4 | convolution fusion | flops 402653184 | bytes 7012352 | tf_op jit(solution)/shard_map/dot_general | solution.py:39
  58.8 14.2 %all_to_all.16 = f32[8,8,768]{2,1,0:T(8,128)S(1)} all-to-all(f32[8,8,768]{2,1,0:T(8,128)S(1)} %fusion.4), channel_id=1, replica_groups=mesh['mod'=8,'row'=16] {'mod'}, dimensions={0} | all-to-all | bytes 393216 | tf_op jit(solution)/shard_map/all_to_all | solution.py:34
  73.1 0.6 reduce_sum.49
  (7 shorter events, 0.0 us)
Async XLA Ops:
  0.0 39.5 %copy-start = (bf16[1,256,4096]{2,1,0:T(8,128)(2,1)S(1)}, bf16[1,256,4096]{2,1,0:T(8,128)(2,1)}, u32[]{:S(2)}) copy-start(bf16[1,256,4096]{2,1,0:T(8,128)(2,1)} %param.12) | copy-start | bytes 6291460
  0.0 10.0 %copy-start.2 = (bf16[1,64,4096]{2,1,0:T(8,128)(2,1)S(1)}, bf16[1,64,4096]{2,1,0:T(8,128)(2,1)}, u32[]{:S(2)}) copy-start(bf16[1,64,4096]{2,1,0:T(8,128)(2,1)} %param.10) | copy-start | bytes 1572868
  0.0 10.0 %copy-start.1 = (bf16[1,1024,4096]{2,1,0:T(8,128)(2,1)S(1)}, bf16[1,1024,4096]{2,1,0:T(8,128)(2,1)}, u32[]{:S(2)}) copy-start(bf16[1,1024,4096]{2,1,0:T(8,128)(2,1)} %param.8) | copy-start | bytes 25165828
  10.0 13.8 %copy-start.3 = (s32[64]{0:T(128)S(1)}, s32[64]{0:T(128)}, u32[]{:S(2)}) copy-start(s32[64]{0:T(128)} %param.15) | copy-start | bytes 772
  16.3 23.3 %all-to-all-start = ((bf16[16,8,4096]{2,1,0:T(8,128)(2,1)}), bf16[16,8,4096]{2,1,0:T(8,128)(2,1)S(1)}, u32[]{:S(2)}, u32[]{:S(2)}) async-start(bf16[16,8,4096]{2,1,0:T(8,128)(2,1)} %broadcast_in_dim.39), calls=%async_computation | async-start | bytes 2097152 | tf_op jit(solution)/shard_map/all_to_all | solution.py:17
where the time goes:
time: 74 us; the launch traced here: 73.7 us
  blocking collectives  27.1 us (37%)
  matrix products  16.8 us (23%)
  waiting for transfers between devices  15.6 us (21%)
  starting transfers between devices  7.58 us (10%)
  other arithmetic  4.36 us (6%)
  local copies, waits for them, and re-layouts  2 us (3%)
    all_to_all x1, waiting for transfers between devices, sent_to_all(): lax.all_to_all(jnp.broadcast_to(array[None], (peers, *array.shape)), axis...  15.6 us
    dot_general x4, matrix products, contract_last(): lax.dot_general(left, right, (((1,), (1,)), ((), ())), preferred_element_...  14.7 us
    all_to_all x1, blocking collectives, sent_and_summed(): lax.all_to_all(pieces, axis, split_axis=0, concat_axis=0, tiled=True)  14.2 us
    all_to_all x1, blocking collectives, sent_to_all(): lax.all_to_all(jnp.broadcast_to(array[None], (peers, *array.shape)), axis...  12.9 us
    all_to_all x1, starting transfers between devices, sent_to_all(): lax.all_to_all(jnp.broadcast_to(array[None], (peers, *array.shape)), axis...  7.58 us
    dot_general x1, matrix products, on_device(): jnp.dot(weighted.reshape(capacity * rank, tok_rows), in_feat, precision=e...  2.16 us
  transfers between devices with their start and end apart: 1, of which 1 were waited for; matrix products, arithmetic and copies ran while one was open for 0% of the time, Pallas kernels for 0%

commit v1 on v0

v1 whole, which is shorter than its diff:
```python
import functools

import jax
import jax.numpy as jnp
from jax import lax
from jax.experimental import pallas as pl
from jax.experimental.pallas import tpu as pltpu
from jax.sharding import PartitionSpec as P

f32, bf16 = jnp.float32, jnp.bfloat16
CAP = 8
LEN_MAX, LEN_MIN = 128, 64
TILES = 4
SIDE = 4


def dot_nt(a, b):
    return lax.dot_general(a, b, (((1,), (1,)), ((), ())), preferred_element_type=f32)


def dot_nn(a, b):
    return lax.dot_general(a, b, (((1,), (0,)), ((), ())), preferred_element_type=f32)


def halves(x):
    hi = x.astype(bf16)
    return hi, (x - hi.astype(f32)).astype(bf16)


def remote(src, dst, send, recv, axis, peer):
    return pltpu.make_async_remote_copy(
        src_ref=src, dst_ref=dst, send_sem=send, recv_sem=recv,
        device_id={axis: peer}, device_id_type=pl.DeviceIdType.MESH,
    )


def row_of(x, y):
    return x * SIDE + y


class Gather:
    def __init__(self, part, send, recv, x, y):
        self.part, self.send, self.recv, self.x, self.y = part, send, recv, x, y
        self.started = []

    def coord(self, h, d):
        x, y = self.x, self.y
        if h == 0:
            return row_of(x, lax.rem(y + d, SIDE))
        return row_of(lax.rem(x + d, SIDE), y)

    def src(self, h, d1, d2):
        if h == 0:
            return row_of(lax.rem(self.x + d2, SIDE), lax.rem(self.y + d1, SIDE))
        return row_of(lax.rem(self.x + d1, SIDE), lax.rem(self.y + d2, SIDE))

    def copy(self, h, e1, e2, f1, f2):
        r = self.src(h, e1, e2)
        k = (h, (e1 - f1) % SIDE, (e2 - f2) % SIDE)
        i = len(self.started)
        return remote(self.part(h, r), self.part(h, r), self.send.at[i], self.recv.at[k[0], k[1], k[2]],
                      "row", self.src(h, f1, f2))

    def begin(self, c):
        c.start()
        self.started.append(c)

    def first(self):
        for d in (1, 3, 2):
            for h in (0, 1):
                self.begin(self.copy(h, 0, 0, d, 0))
        self.forward(0)

    def forward(self, e):
        for d in (1, 3, 2):
            for h in (0, 1):
                self.begin(self.copy(h, e, 0, 0, d))

    def wait(self, e1, e2):
        for h in (0, 1):
            r = self.src(h, e1, e2)
            remote(self.part(h, r), self.part(h, r), self.send.at[0], self.recv.at[h, e1, e2], "row",
                   self.coord(h, 1)).wait_recv()

    def finish(self):
        for c in self.started:
            c.wait_send()


def kernel(lens_ref, owners_ref, act_h, grad_h, pin_h, pout_h, curv_h, store_h, out_ref,
           act, grad, pin, pout, curv, store, acc, spread, feats, pres, score, parts,
           in_sem, send1, recv1, send2, recv2, send3, recv3):
    mods, rows = lax.axis_size("mod"), lax.axis_size("row")
    mod_id, row_id = lax.axis_index("mod"), lax.axis_index("row")
    x, y = row_id // SIDE, lax.rem(row_id, SIDE)
    tokens, width = act.shape
    rank = pin.shape[0]
    queries = lens_ref.shape[1]
    tile = tokens // TILES

    copies = {}
    def fetch(name, src, dst, i):
        copies[name] = pltpu.make_async_copy(src, dst, in_sem.at[i])
        copies[name].start()
    fetch("pin", pin_h.at[0], pin, 0)
    fetch("act0", act_h.at[0, pl.ds(0, tile)], act.at[pl.ds(0, tile)], 1)
    fetch("pout", pout_h.at[0], pout, 2)
    fetch("grad0", grad_h.at[0, pl.ds(0, tile)], grad.at[pl.ds(0, tile)], 3)
    for t in range(1, TILES):
        at = pl.ds(t * tile, tile)
        fetch(f"act{t}", act_h.at[0, at], act.at[at], 2 + 2 * t)
        fetch(f"grad{t}", grad_h.at[0, at], grad.at[at], 3 + 2 * t)
    fetch("curv", curv_h.at[0], curv, 2 + 2 * TILES)
    fetch("store", store_h.at[0], store, 3 + 2 * TILES)

    barrier = pltpu.get_barrier_semaphore()
    for d in range(1, rows):
        pl.semaphore_signal(barrier, inc=1, device_id={"row": lax.rem(row_id + d, rows)}, device_id_type=pl.DeviceIdType.MESH)
    for d in range(1, mods):
        pl.semaphore_signal(barrier, inc=1, device_id={"mod": lax.rem(mod_id + d, mods)}, device_id_type=pl.DeviceIdType.MESH)

    i0 = lax.broadcasted_iota(jnp.int32, (queries, queries), 0)
    i1 = lax.broadcasted_iota(jnp.int32, (queries, queries), 1)
    own_r = owners_ref[...]
    len_r = lens_ref[...]
    own_rb = jnp.broadcast_to(own_r, (queries, queries))
    len_rb = jnp.broadcast_to(len_r, (queries, queries))
    own_c = jnp.sum(jnp.where(i0 == i1, own_rb, 0), axis=1, keepdims=True)
    len_c = jnp.sum(jnp.where(i0 == i1, len_rb, 0), axis=1, keepdims=True)
    same = own_c == own_rb
    before_c = same & (i1 < i0)
    before_r = same & (i0 < i1)
    rank_c = jnp.sum(jnp.where(before_c, 1, 0), axis=1, keepdims=True)
    rank_r = jnp.sum(jnp.where(before_r, 1, 0), axis=0, keepdims=True)
    off_r = jnp.sum(jnp.where(before_r, jnp.broadcast_to(len_c, (queries, queries)), 0), axis=0, keepdims=True)
    s0 = lax.broadcasted_iota(jnp.int32, (CAP, queries), 0)
    chosen = (jnp.broadcast_to(rank_r, (CAP, queries)) == s0) & (jnp.broadcast_to(own_r, (CAP, queries)) == row_id)
    begin = jnp.sum(jnp.where(chosen, jnp.broadcast_to(off_r, (CAP, queries)), 0), axis=1, keepdims=True)
    count = jnp.sum(jnp.where(chosen, jnp.broadcast_to(len_r, (CAP, queries)), 0), axis=1, keepdims=True)
    end = begin + count
    slot_c = own_c * CAP + rank_c
    g1 = lax.broadcasted_iota(jnp.int32, (queries, rows * CAP), 1)
    placer = jnp.where(jnp.broadcast_to(slot_c, (queries, rows * CAP)) == g1, 1.0, 0.0).astype(bf16)

    fresh = [True] * CAP
    copies["pin"].wait()
    copies["pout"].wait()
    for t in range(TILES):
        at = pl.ds(t * tile, tile)
        copies[f"act{t}"].wait()
        fin = dot_nt(act[at, :], pin[...])
        copies[f"grad{t}"].wait()
        fout = dot_nt(grad[at, :], pout[...])
        in_hi, in_lo = halves(fin)
        right = jnp.concatenate([in_hi, in_lo, in_hi], axis=0)
        right = jnp.concatenate([right, right], axis=1)
        fout_t = fout.T
        pos = lax.broadcasted_iota(jnp.int32, (CAP, tile), 1) + t * tile
        member = (pos >= begin) & (pos < end)
        member = jnp.where(member, 1.0, 0.0)
        slots = [s for s in range(CAP) if LEN_MIN * s < (t + 1) * tile and LEN_MAX * (s + 1) > t * tile]
        for s in slots:
            w = fout_t * member[s:s + 1, :]
            w_hi, w_lo = halves(w)
            left = jnp.concatenate([w_hi, w_hi, w_lo], axis=1)
            g = dot_nn(left, right)
            if fresh[s]:
                acc[s] = g
                fresh[s] = False
            else:
                acc[s] = acc[s] + g
    lane = lax.broadcasted_iota(jnp.int32, (rank // 2, 2 * rank), 1)
    for s in range(CAP):
        even = acc[s, pl.ds(0, rank // 2, stride=2), :]
        odd = acc[s, pl.ds(1, rank // 2, stride=2), :]
        spread[:, s, :] = jnp.where(lane < rank, even, odd)
    for r in range(rank // 2):
        feats[row_id, :, r * 128:(r + 1) * 128] = spread[r].astype(bf16)

    pl.semaphore_wait(barrier, rows - 1 + mods - 1)

    half = rank * rank // 2
    g1_ = Gather(lambda h, r: feats.at[r, :, pl.ds(h * half, half)], send1, recv1, x, y)
    g1_.first()
    for d in (1, 3, 2):
        g1_.wait(d, 0)
        g1_.forward(d)
    for e2 in (1, 3, 2):
        for e1 in (0, 1, 3, 2):
            g1_.wait(e1, e2)

    copies["curv"].wait()
    whole = feats[...].reshape(rows * CAP, rank * rank)
    pre = dot_nt(whole, curv[...]).astype(bf16)
    pre = dot_nn(placer, pre).astype(bf16)
    pres[row_id] = pre

    hq = queries // 2
    g2_ = Gather(lambda h, r: pres.at[r, pl.ds(h * hq, hq)], send2, recv2, x, y)
    g2_.first()
    for d in (1, 3, 2):
        g2_.wait(d, 0)
        g2_.forward(d)
    for e2 in (1, 3, 2):
        for e1 in (0, 1, 3, 2):
            g2_.wait(e1, e2)

    copies["store"].wait()
    cols = pres.shape[2]
    total = None
    for j in range(rows):
        part = dot_nt(pres[j], store[:, j * cols:(j + 1) * cols])
        total = part if total is None else total + part
    score[...] = total.reshape(score.shape)
    parts[mod_id] = score[mod_id]
    sent = []
    for d in range(1, mods):
        peer = lax.rem(mod_id + d, mods)
        c = remote(score.at[peer], parts.at[mod_id], send3.at[d], recv3.at[d], "mod", peer)
        c.start()
        sent.append(c)
    for c in sent:
        c.wait()
    summed = parts[0]
    for m in range(1, mods):
        summed = summed + parts[m]
    out_ref[...] = summed
    g1_.finish()
    g2_.finish()


def on_device(activations, out_grads, in_projection, out_projection, inv_curvature, store_grads, lengths, owners):
    _, tokens, width = activations.shape
    rank = in_projection.shape[1]
    queries = lengths.shape[0]
    mods, rows = lax.axis_size("mod"), lax.axis_size("row")
    held, depth = store_grads.shape[1], store_grads.shape[2]
    share = inv_curvature.shape[1]
    hbm = pl.BlockSpec(memory_space=pl.ANY)
    vmem = pl.BlockSpec(memory_space=pltpu.VMEM)
    dma = pltpu.SemaphoreType.DMA
    return pl.pallas_call(
        kernel,
        out_shape=jax.ShapeDtypeStruct((queries // mods, held), f32),
        in_specs=[vmem, vmem] + [hbm] * 6,
        out_specs=vmem,
        scratch_shapes=[
            pltpu.VMEM((tokens, width), bf16),
            pltpu.VMEM((tokens, width), bf16),
            pltpu.VMEM((rank, width), bf16),
            pltpu.VMEM((rank, width), bf16),
            pltpu.VMEM((share, depth), bf16),
            pltpu.VMEM((held, depth), bf16),
            pltpu.VMEM((CAP, rank, 2 * rank), f32),
            pltpu.VMEM((rank // 2, CAP, 2 * rank), f32),
            pltpu.VMEM((rows, CAP, rank * rank), bf16),
            pltpu.VMEM((rows, queries, share), bf16),
            pltpu.VMEM((mods, queries // mods, held), f32),
            pltpu.VMEM((mods, queries // mods, held), f32),
            dma((4 + 2 * TILES,)),
            dma((30,)), dma((2, SIDE, SIDE)),
            dma((30,)), dma((2, SIDE, SIDE)),
            dma((mods,)), dma((mods,)),
        ],
        compiler_params=pltpu.CompilerParams(collective_id=0, has_side_effects=True, vmem_limit_bytes=60 * 1024 * 1024),
    )(lengths.reshape(1, queries), owners.reshape(1, queries), activations, out_grads, in_projection,
      out_projection, inv_curvature, store_grads)


def solution(mesh):
    return jax.shard_map(
        on_device,
        mesh=mesh,
        in_specs=(
            P("mod", "row", None),
            P("mod", "row", None),
            P("mod", None, None),
            P("mod", None, None),
            P("mod", "row", None),
            P("mod", "row", None),
            P(),
            P(),
        ),
        out_specs=P("mod", "row"),
        check_vma=False,
    )
```

time: 74 us -> 48.8 us (0.66)
  Pallas kernels: 0 us -> 47.3 us
  blocking collectives: 27.1 us -> 0 us
  matrix products: 16.8 us -> 0 us
  waiting for transfers between devices: 15.6 us -> 0 us
  starting transfers between devices: 7.58 us -> 0 us
  other arithmetic: 4.36 us -> 0 us
    pallas_call x0 -> x1, Pallas kernels: none -> 47.3 us  [on_device(): pl.pallas_call(kernel, out_shape=jax.ShapeDtypeStruct((queries // mods, h...]
    all_to_all x2 -> x0, blocking collectives: 27.1 us -> none  [the longest x1 14.2 us: sent_and_summed(): lax.all_to_all(pieces, axis, split_axis=0, concat_axis=0, tiled=True)]
    dot_general x5 -> x0, matrix products: 16.8 us -> none  [the longest x4 14.7 us: contract_last(): lax.dot_general(left, right, (((1,), (1,)), ((), ())), preferred_element_...]
    all_to_all x1 -> x0, waiting for transfers between devices: 15.6 us -> none  [sent_to_all(): lax.all_to_all(jnp.broadcast_to(array[None], (peers, *array.shape)), axis...]
    all_to_all x1 -> x0, starting transfers between devices: 7.58 us -> none  [sent_to_all(): lax.all_to_all(jnp.broadcast_to(array[None], (peers, *array.shape)), axis...]
    reduce_sum x3 -> x0, other arithmetic: 2.71 us -> none  [the longest x1 1.07 us: on_device(): slot_length = jnp.sum(jnp.where(chosen, lengths[None, :], 0), axis=1)]
    unnamed x8 -> x1, local copies, waits for them, and re-layouts: 0.02 us -> 1.35 us
    eq x1 -> x0, other arithmetic: 1.3 us -> none  [on_device(): owned_here = owners == row_id]
  transfers between devices with their start and end apart: 1 -> 0, of which waited for: 1 -> 0; matrix products, arithmetic and copies ran while one was open for 0% -> 0% of each run, Pallas kernels for 0% -> 0%
where the time goes in v1:
time: 48.8 us; the launch traced here: 48.6 us
  Pallas kernels  47.3 us (97%)
  local copies, waits for them, and re-layouts  1.35 us (3%)
    pallas_call x1, Pallas kernels, on_device(): pl.pallas_call(kernel, out_shape=jax.ShapeDtypeStruct((queries // mods, h...  47.3 us
    unnamed x1, local copies, waits for them, and re-layouts  1.35 us

profile of v1, /device:TPU:1, one launch (start us, length us, event | category | flops | bytes accessed | tf_op | source)
XLA Modules:
  0.0 48.6 jit_solution(3843994019995146812)
XLA Ops:
  0.0 47.3 %shard_map.82 = f32[8,768]{1,0:T(8,128)} custom-call(s32[1,64]{1,0:T(1,128)} %bitcast.2, s32[1,64]{1,0:T(1,128)} %bitcast.3, bf16[1,1024,4096]{2,1,0:T(8,128)(2,1)} %act_h.1, bf16[1,1024,4096]{2,1,0:T(8,128)(2,1)} %grad_h.1, bf16[1,64,4096]{2,1,0:T(8,128)(2,1)} %pin_h.1, bf16[1,64,4096]{2,1,0:T(8,128)(2,1)} %pout_h.1, bf16[1,256,4096]{2,1,0:T(8,128)(2,1)} %curv_h.1, ...), custom_call_target="tpu_custom_call" | custom-call | tf_op jit(solution)/shard_map/pallas_call | solution.py:242
  47.3 1.3 %copy.10 = f32[8,768]{1,0:T(8,128)} copy(f32[8,768]{1,0:T(8,128)} %shard_map.82) | data formatting | bytes 49152

commit v2 on v0

v2 whole, which is shorter than its diff:
```python
import jax
import jax.numpy as jnp
from jax import lax
from jax.experimental import pallas as pl
from jax.experimental.pallas import tpu as pltpu
from jax.sharding import PartitionSpec as P

f32, bf16 = jnp.float32, jnp.bfloat16
CAP = 8
LEN_MAX, LEN_MIN = 128, 64
TILES = 4
PAIR = CAP // TILES
SIDE = 4


def dot_nt(a, b):
    return lax.dot_general(a, b, (((1,), (1,)), ((), ())), preferred_element_type=f32)


def dot_nn(a, b):
    return lax.dot_general(a, b, (((1,), (0,)), ((), ())), preferred_element_type=f32)


def halves(x):
    hi = x.astype(bf16)
    return hi, (x - hi.astype(f32)).astype(bf16)


def remote(src, dst, send, recv, axis, peer):
    return pltpu.make_async_remote_copy(
        src_ref=src, dst_ref=dst, send_sem=send, recv_sem=recv,
        device_id={axis: peer}, device_id_type=pl.DeviceIdType.MESH,
    )


def taken(ref, sem):
    pltpu.make_async_copy(ref, ref, sem).wait()


class Gather:
    def __init__(self, own, part, blocks, sems, x, y):
        self.own, self.part, self.blocks, self.x, self.y = own, part, blocks, x, y
        self.send, self.near, self.far, self.rest = (sems.at[i] for i in range(4))

    def at(self, h, d1, d2):
        dx, dy = (d2, d1) if h == 0 else (d1, d2)
        return lax.rem(self.x + dx, SIDE) * SIDE + lax.rem(self.y + dy, SIDE)

    def first(self):
        for d, sem in ((1, self.near), (3, self.near), (2, self.far)):
            for h in (0, 1):
                place = self.part(h, self.at(h, 0, 0))
                remote(self.own(h), place, self.send, sem, "row", self.at(h, d, 0)).start()
        for h in (0, 1):
            self.onward(h, 0, self.own(h))

    def onward(self, h, e, block):
        place = self.part(h, self.at(h, e, 0))

        def to(d, _):
            remote(block, place, self.send, self.rest, "row", self.at(h, 0, d)).start()
            return 0
        lax.fori_loop(1, SIDE, to, 0)

    def forward(self):
        taken(self.blocks(2), self.near)
        for h in (0, 1):
            for e in (1, 3):
                self.onward(h, e, self.part(h, self.at(h, e, 0)))
        taken(self.blocks(1), self.far)
        for h in (0, 1):
            self.onward(h, 2, self.part(h, self.at(h, 2, 0)))

    def wait(self):
        taken(self.blocks(12), self.rest)

    def finish(self):
        taken(self.blocks(15), self.send)


class Direct:
    def __init__(self, own, part, blocks, send, recv, x, y):
        self.own, self.part, self.blocks, self.send, self.recv, self.x, self.y = own, part, blocks, send, recv, x, y

    def first(self):
        def step(i, _):
            dx, dy = i // SIDE, lax.rem(i, SIDE)
            remote(self.own, self.part, self.send, self.recv.at[lax.rem(SIDE - dx, SIDE)], "row",
                   lax.rem(self.x + dx, SIDE) * SIDE + lax.rem(self.y + dy, SIDE)).start()
            return 0
        lax.fori_loop(1, SIDE * SIDE, step, 0)

    def wait_x(self, dx):
        @pl.when(dx == 0)
        def _():
            taken(self.blocks(SIDE - 1), self.recv.at[0])

        @pl.when(dx != 0)
        def _():
            taken(self.blocks(SIDE), self.recv.at[dx])

    def finish(self):
        taken(self.blocks(SIDE * SIDE - 1), self.send)


def kernel(lens_h, owners_h, act_h, grad_h, pin_h, pout_h, curv_h, store_h, out_ref,
           lens, owners, rowsv, proj, curv, store, res, limits, acc, spread, ready, feats, pres, total, score, parts,
           in_sem, own_sem, sems1, sems2, last1, last2, sems3):
    mods, rows = lax.axis_size("mod"), lax.axis_size("row")
    mod_id, row_id = lax.axis_index("mod"), lax.axis_index("row")
    x, y = row_id // SIDE, lax.rem(row_id, SIDE)
    tokens, width = rowsv.shape[1:]
    rank = proj.shape[1]
    entries = rank * rank
    queries = lens_h.shape[1]
    share = curv.shape[0]
    tile = tokens // TILES

    tile_sem, proj_sem, late_sem, small_sem = in_sem
    small = [pltpu.make_async_copy(lens_h, lens, small_sem.at[0]), pltpu.make_async_copy(owners_h, owners, small_sem.at[1])]
    projs = [pltpu.make_async_copy(h.at[0], proj.at[m], proj_sem.at[m]) for m, h in enumerate((pin_h, pout_h))]
    late = [pltpu.make_async_copy(curv_h.at[0], curv, late_sem.at[0]), pltpu.make_async_copy(store_h.at[0], store, late_sem.at[1])]

    def tile_copy(m, t):
        at = pl.ds(pl.multiple_of(t * tile, tile), tile)
        return pltpu.make_async_copy((act_h, grad_h)[m].at[0, at], rowsv.at[m, at], tile_sem.at[m, t])

    small[0].start()
    small[1].start()
    for m in (0, 1):
        projs[m].start()
        tile_copy(m, 0).start()

    def fetch_tile(t, _):
        tile_copy(0, t).start()
        tile_copy(1, t).start()
        return 0
    lax.fori_loop(1, TILES, fetch_tile, 0)

    barrier = pltpu.get_barrier_semaphore()

    def greet(axis, me, n):
        def step(d, _):
            pl.semaphore_signal(barrier, inc=1, device_id={axis: lax.rem(me + d, n)}, device_id_type=pl.DeviceIdType.MESH)
            return 0
        lax.fori_loop(1, n, step, 0)
    greet("row", row_id, rows)
    greet("mod", mod_id, mods)

    small[0].wait()
    small[1].wait()
    i0 = lax.broadcasted_iota(jnp.int32, (queries, queries), 0)
    i1 = lax.broadcasted_iota(jnp.int32, (queries, queries), 1)
    own_r = owners[...]
    len_r = lens[...]
    own_rb = jnp.broadcast_to(own_r, (queries, queries))
    len_rb = jnp.broadcast_to(len_r, (queries, queries))
    own_c = jnp.sum(jnp.where(i0 == i1, own_rb, 0), axis=1, keepdims=True)
    len_c = jnp.sum(jnp.where(i0 == i1, len_rb, 0), axis=1, keepdims=True)
    same = own_c == own_rb
    before_c = same & (i1 < i0)
    before_r = same & (i0 < i1)
    rank_c = jnp.sum(jnp.where(before_c, 1, 0), axis=1, keepdims=True)
    rank_r = jnp.sum(jnp.where(before_r, 1, 0), axis=0, keepdims=True)
    off_r = jnp.sum(jnp.where(before_r, jnp.broadcast_to(len_c, (queries, queries)), 0), axis=0, keepdims=True)
    s0 = lax.broadcasted_iota(jnp.int32, (CAP, queries), 0)
    chosen = (jnp.broadcast_to(rank_r, (CAP, queries)) == s0) & (jnp.broadcast_to(own_r, (CAP, queries)) == row_id)
    begin = jnp.sum(jnp.where(chosen, jnp.broadcast_to(off_r, (CAP, queries)), 0), axis=1, keepdims=True)
    count = jnp.sum(jnp.where(chosen, jnp.broadcast_to(len_r, (CAP, queries)), 0), axis=1, keepdims=True)
    limits[0] = jnp.broadcast_to(begin, limits.shape[1:])
    limits[1] = jnp.broadcast_to(begin + count, limits.shape[1:])
    slot_c = (rank_c // PAIR) * (rows * PAIR) + own_c * PAIR + rank_c % PAIR

    def row_pair(r):
        return pl.ds(pl.multiple_of(r * PAIR, PAIR), PAIR)

    LAST = TILES - 1

    def features(t):
        half = entries // 2
        return Gather(lambda h: ready.at[t, pl.ds(0, PAIR), pl.ds(h * half, half)],
                      lambda h, r: feats.at[t, row_pair(r), pl.ds(h * half, half)],
                      lambda n: pres.at[t, pl.ds(0, n)], sems1.at[t], x, y)

    last_features = Direct(ready.at[LAST, pl.ds(0, PAIR)], feats.at[LAST, row_pair(row_id)],
                           lambda n: pres.at[LAST, pl.ds(0, n)], last1.at[SIDE], last1, x, y)

    def pre_rows(t):
        half = rows * PAIR // 2
        return Gather(lambda h: pres.at[t, row_id, pl.ds(h * half, half)],
                      lambda h, r: pres.at[t, r, pl.ds(h * half, half)],
                      lambda n: pres.at[t, pl.ds(0, n)], sems2.at[t], x, y)

    last_pre_rows = Direct(pres.at[LAST, row_id], pres.at[LAST, row_id],
                           lambda n: pres.at[LAST, pl.ds(0, n)], last2.at[SIDE], last2, x, y)

    def own(t):
        return pltpu.make_async_copy(ready.at[t, pl.ds(0, PAIR)], feats.at[t, row_pair(row_id)], own_sem.at[t])

    acc[...] = jnp.zeros_like(acc)
    projs[0].wait()
    projs[1].wait()

    def token_tile(t, _):
        at = pl.ds(pl.multiple_of(t * tile, tile), tile)

        def side(m, _):
            pltpu.make_async_copy(act_h.at[0, at], rowsv.at[m, at], tile_sem.at[m, t]).wait()
            res[m] = dot_nt(rowsv[m, at, :], proj[m])
            return 0
        lax.fori_loop(0, 2, side, 0)

        @pl.when(t == 1)
        def _():
            late[0].start()
            late[1].start()

        in_hi, in_lo = halves(res[0])
        in_hi = jnp.concatenate([in_hi, in_hi], axis=1)
        in_lo = jnp.concatenate([in_lo, in_lo], axis=1)
        right = jnp.concatenate([jnp.concatenate([in_hi, in_lo], axis=1)] * 2, axis=0)
        fout_t = res[1].T
        pos = lax.broadcasted_iota(jnp.int32, (CAP, tile), 1) + t * tile
        member = jnp.where((pos >= limits[0]) & (pos < limits[1]), 1.0, 0.0)
        member = member.astype(bf16)
        out_hi, out_lo = halves(fout_t)
        left = []
        for s in range(CAP):
            m = jnp.broadcast_to(member[s:s + 1, :], out_hi.shape)
            left.append(jnp.concatenate([out_hi * m, out_lo * m], axis=1))
        g = dot_nn(jnp.concatenate(left, axis=0), right)
        acc[...] = acc[...] + (g[:, :2 * rank] + g[:, 2 * rank:])
        lane = lax.broadcasted_iota(jnp.int32, (rank // 2, 2 * rank), 1)
        for p in range(PAIR):
            base = pl.multiple_of((t * PAIR + p) * rank, rank)
            even = acc[pl.ds(base, rank // 2, stride=2), :]
            odd = acc[pl.ds(base + 1, rank // 2, stride=2), :]
            spread[:, p, :] = jnp.where(lane < rank, even, odd)
        for r in range(rank // 2):
            ready[t, 0:PAIR, r * 128:(r + 1) * 128] = spread[r, 0:PAIR, :].astype(bf16)

        @pl.when(t == 0)
        def _():
            pl.semaphore_wait(barrier, rows - 1 + mods - 1)
        own(t).start()

        @pl.when(t != LAST)
        def _():
            features(t).first()

        @pl.when(t == LAST)
        def _():
            last_features.first()

        @pl.when(t >= 2)
        def _():
            features(t - 2).forward()
        return 0
    lax.fori_loop(0, TILES, token_tile, 0)

    late[0].wait()

    def precondition(t):
        own(t).wait()
        chunk = 4 * share

        def step(k, sums):
            at = pl.ds(pl.multiple_of(k * chunk, chunk), chunk)
            return sums + dot_nt(feats[t, :, at], curv[:, at])
        sums = lax.fori_loop(0, entries // chunk, step, jnp.zeros((rows * PAIR, share), f32))
        pres[t, row_id] = sums.astype(bf16)

    def batch(t, _):
        @pl.when(t == 1)
        def _():
            features(2).forward()

        features(t).wait()
        precondition(t)
        pre_rows(t).first()

        @pl.when(t >= 1)
        def _():
            pre_rows(t - 1).forward()
        return 0
    lax.fori_loop(0, LAST, batch, 0)

    def arrived(dx, _):
        last_features.wait_x(dx)
        return 0
    lax.fori_loop(0, SIDE, arrived, 0)
    precondition(LAST)
    last_pre_rows.first()
    pre_rows(LAST - 1).forward()

    late[1].wait()
    total[...] = jnp.zeros_like(total)

    def here(t, _):
        pre_rows(t).wait()
        return 0
    lax.fori_loop(0, LAST, here, 0)

    def source(dx, _):
        last_pre_rows.wait_x(dx)
        r = lax.rem(x + dx, SIDE) * SIDE
        left = [jnp.concatenate([pres[t, r + k] for t in range(TILES)], axis=0) for k in range(SIDE)]
        right = store[:, pl.ds(pl.multiple_of(r * share, SIDE * share), SIDE * share)]
        total[...] = total[...] + dot_nt(jnp.concatenate(left, axis=1), right)
        return 0
    lax.fori_loop(0, SIDE, source, 0)

    g1 = lax.broadcasted_iota(jnp.int32, (queries, rows * CAP), 1)
    placer = jnp.where(jnp.broadcast_to(slot_c, (queries, rows * CAP)) == g1, 1.0, 0.0).astype(bf16)
    score[...] = dot_nn(placer, total[...].astype(bf16)).astype(bf16).reshape(score.shape)

    def send(d, _):
        peer = lax.rem(mod_id + d, mods)
        remote(score.at[peer], parts.at[mod_id], sems3.at[0], sems3.at[1], "mod", peer).start()
        return 0
    lax.fori_loop(1, mods, send, 0)
    parts[mod_id] = score[mod_id]
    taken(parts.at[pl.ds(0, mods - 1)], sems3.at[1])
    summed = parts[0].astype(f32)
    for m in range(1, mods):
        summed = summed + parts[m].astype(f32)
    out_ref[...] = summed

    def finish(t, _):
        features(t).finish()
        pre_rows(t).finish()
        return 0
    lax.fori_loop(0, LAST, finish, 0)
    last_features.finish()
    last_pre_rows.finish()
    taken(score.at[pl.ds(0, mods - 1)], sems3.at[0])


def on_device(activations, out_grads, in_projection, out_projection, inv_curvature, store_grads, lengths, owners):
    _, tokens, width = activations.shape
    rank = in_projection.shape[1]
    queries = lengths.shape[0]
    mods, rows = lax.axis_size("mod"), lax.axis_size("row")
    held, depth = store_grads.shape[1], store_grads.shape[2]
    share = inv_curvature.shape[1]
    hbm = pl.BlockSpec(memory_space=pl.ANY)
    vmem = pl.BlockSpec(memory_space=pltpu.VMEM)
    dma = pltpu.SemaphoreType.DMA
    return pl.pallas_call(
        kernel,
        out_shape=jax.ShapeDtypeStruct((queries // mods, held), f32),
        in_specs=[hbm] * 8,
        out_specs=vmem,
        scratch_shapes=[
            pltpu.VMEM((1, queries), jnp.int32),
            pltpu.VMEM((1, queries), jnp.int32),
            pltpu.VMEM((2, tokens, width), bf16),
            pltpu.VMEM((2, rank, width), bf16),
            pltpu.VMEM((share, depth), bf16),
            pltpu.VMEM((held, depth), bf16),
            pltpu.VMEM((2, tokens // TILES, rank), f32),
            pltpu.VMEM((2, CAP, tokens // TILES), jnp.int32),
            pltpu.VMEM((CAP * rank, 2 * rank), f32),
            pltpu.VMEM((rank // 2, CAP, 2 * rank), f32),
            pltpu.VMEM((TILES, CAP, rank * rank), bf16),
            pltpu.VMEM((TILES, rows * PAIR, rank * rank), bf16),
            pltpu.VMEM((TILES, rows, rows * PAIR, share), bf16),
            pltpu.VMEM((rows * CAP, held), f32),
            pltpu.VMEM((mods, queries // mods, held), bf16),
            pltpu.VMEM((mods, queries // mods, held), bf16),
            (dma((2, TILES)), dma((2,)), dma((2,)), dma((2,))),
            dma((TILES,)),
            dma((TILES - 1, 4)), dma((TILES - 1, 4)),
            dma((SIDE + 1,)), dma((SIDE + 1,)),
            dma((2,)),
        ],
        compiler_params=pltpu.CompilerParams(collective_id=0, has_side_effects=True, vmem_limit_bytes=60 * 1024 * 1024),
    )(lengths.reshape(1, queries), owners.reshape(1, queries), activations, out_grads, in_projection,
      out_projection, inv_curvature, store_grads)


def solution(mesh):
    return jax.shard_map(
        on_device,
        mesh=mesh,
        in_specs=(
            P("mod", "row", None),
            P("mod", "row", None),
            P("mod", None, None),
            P("mod", None, None),
            P("mod", "row", None),
            P("mod", "row", None),
            P(),
            P(),
        ),
        out_specs=P("mod", "row"),
        check_vma=False,
    )
```

time: 74 us -> 42.9 us (0.58)
  Pallas kernels: 0 us -> 41.4 us
  blocking collectives: 27.1 us -> 0 us
  matrix products: 16.8 us -> 0 us
  waiting for transfers between devices: 15.6 us -> 0 us
  starting transfers between devices: 7.58 us -> 0 us
  other arithmetic: 4.36 us -> 0 us
    pallas_call x0 -> x1, Pallas kernels: none -> 41.4 us  [on_device(): pl.pallas_call(kernel, out_shape=jax.ShapeDtypeStruct((queries // mods, h...]
    all_to_all x2 -> x0, blocking collectives: 27.1 us -> none  [the longest x1 14.2 us: sent_and_summed(): lax.all_to_all(pieces, axis, split_axis=0, concat_axis=0, tiled=True)]
    dot_general x5 -> x0, matrix products: 16.8 us -> none  [the longest x4 14.7 us: contract_last(): lax.dot_general(left, right, (((1,), (1,)), ((), ())), preferred_element_...]
    all_to_all x1 -> x0, waiting for transfers between devices: 15.6 us -> none  [sent_to_all(): lax.all_to_all(jnp.broadcast_to(array[None], (peers, *array.shape)), axis...]
    all_to_all x1 -> x0, starting transfers between devices: 7.58 us -> none  [sent_to_all(): lax.all_to_all(jnp.broadcast_to(array[None], (peers, *array.shape)), axis...]
    reduce_sum x3 -> x0, other arithmetic: 2.71 us -> none  [the longest x1 1.07 us: on_device(): slot_length = jnp.sum(jnp.where(chosen, lengths[None, :], 0), axis=1)]
    unnamed x8 -> x1, local copies, waits for them, and re-layouts: 0.02 us -> 1.35 us
    eq x1 -> x0, other arithmetic: 1.3 us -> none  [on_device(): owned_here = owners == row_id]
  transfers between devices with their start and end apart: 1 -> 0, of which waited for: 1 -> 0; matrix products, arithmetic and copies ran while one was open for 0% -> 0% of each run, Pallas kernels for 0% -> 0%
where the time goes in v2:
time: 42.9 us; the launch traced here: 42.7 us
  Pallas kernels  41.4 us (97%)
  local copies, waits for them, and re-layouts  1.35 us (3%)
    pallas_call x1, Pallas kernels, on_device(): pl.pallas_call(kernel, out_shape=jax.ShapeDtypeStruct((queries // mods, h...  41.4 us
    unnamed x1, local copies, waits for them, and re-layouts  1.35 us

profile of v2, /device:TPU:1, one launch (start us, length us, event | category | flops | bytes accessed | tf_op | source)
XLA Modules:
  0.0 42.7 jit_solution(3912892080614847513)
XLA Ops:
  0.0 41.4 %shard_map.82 = f32[8,768]{1,0:T(8,128)} custom-call(s32[1,64]{1,0:T(1,128)} %bitcast.2, s32[1,64]{1,0:T(1,128)} %bitcast.3, bf16[1,1024,4096]{2,1,0:T(8,128)(2,1)} %act_h.1, bf16[1,1024,4096]{2,1,0:T(8,128)(2,1)} %grad_h.1, bf16[1,64,4096]{2,1,0:T(8,128)(2,1)} %pin_h.1, bf16[1,64,4096]{2,1,0:T(8,128)(2,1)} %pout_h.1, bf16[1,256,4096]{2,1,0:T(8,128)(2,1)} %curv_h.1, ...), custom_call_target="tpu_custom_call" | custom-call | tf_op jit(solution)/shard_map/pallas_call | solution.py:349
  41.4 1.3 %copy.10 = f32[8,768]{1,0:T(8,128)} copy(f32[8,768]{1,0:T(8,128)} %shard_map.82) | data formatting | bytes 49152

commit v3 on v2

--- a/solution.py
+++ b/solution.py
@@ -9,8 +9,11 @@
 CAP = 8
 LEN_MAX, LEN_MIN = 128, 64
 TILES = 4
+RELAYED = 1
 PAIR = CAP // TILES
 SIDE = 4
+FAR_FIRST = sorted(((dx, dy) for dx in range(SIDE) for dy in range(SIDE) if dx or dy),
+                   key=lambda d: -sum(min(c, SIDE - c) for c in d))
 
 
 def dot_nt(a, b):
@@ -62,11 +65,13 @@
             return 0
         lax.fori_loop(1, SIDE, to, 0)
 
-    def forward(self):
+    def forward_near(self):
         taken(self.blocks(2), self.near)
         for h in (0, 1):
             for e in (1, 3):
                 self.onward(h, e, self.part(h, self.at(h, e, 0)))
+
+    def forward_far(self):
         taken(self.blocks(1), self.far)
         for h in (0, 1):
             self.onward(h, 2, self.part(h, self.at(h, 2, 0)))
@@ -83,12 +88,13 @@
         self.own, self.part, self.blocks, self.send, self.recv, self.x, self.y = own, part, blocks, send, recv, x, y
 
     def first(self):
-        def step(i, _):
-            dx, dy = i // SIDE, lax.rem(i, SIDE)
-            remote(self.own, self.part, self.send, self.recv.at[lax.rem(SIDE - dx, SIDE)], "row",
+        for dx, dy in FAR_FIRST:
+            recv = self.recv.at[(SIDE - dx) % SIDE] if len(self.recv.shape) else self.recv
+            remote(self.own, self.part, self.send, recv, "row",
                    lax.rem(self.x + dx, SIDE) * SIDE + lax.rem(self.y + dy, SIDE)).start()
-            return 0
-        lax.fori_loop(1, SIDE * SIDE, step, 0)
+
+    def wait(self):
+        taken(self.blocks(SIDE * SIDE - 1), self.recv)
 
     def wait_x(self, dx):
         @pl.when(dx == 0)
@@ -104,7 +110,7 @@
 
 
 def kernel(lens_h, owners_h, act_h, grad_h, pin_h, pout_h, curv_h, store_h, out_ref,
-           lens, owners, rowsv, proj, curv, store, res, limits, acc, spread, ready, feats, pres, total, score, parts,
+           lens, owners, rowsv, proj, curv, store, res, limits, acc, spread, ready, feats, pres, last_pres, late_hot, final_hot, total, score, parts,
            in_sem, own_sem, sems1, sems2, last1, last2, sems3):
     mods, rows = lax.axis_size("mod"), lax.axis_size("row")
     mod_id, row_id = lax.axis_index("mod"), lax.axis_index("row")
@@ -115,6 +121,7 @@
     queries = lens_h.shape[1]
     share = curv.shape[0]
     tile = tokens // TILES
+    LAST = TILES - 1
 
     tile_sem, proj_sem, late_sem, small_sem = in_sem
     small = [pltpu.make_async_copy(lens_h, lens, small_sem.at[0]), pltpu.make_async_copy(owners_h, owners, small_sem.at[1])]
@@ -170,29 +177,48 @@
     limits[0] = jnp.broadcast_to(begin, limits.shape[1:])
     limits[1] = jnp.broadcast_to(begin + count, limits.shape[1:])
     slot_c = (rank_c // PAIR) * (rows * PAIR) + own_c * PAIR + rank_c % PAIR
+    early_rows = late_rows = rows * CAP // 2
+    late_most = queries // 2
+    is_late_r, is_late_c = rank_r >= CAP // 2, rank_c >= CAP // 2
+    place_c = jnp.sum(jnp.where((i1 < i0) & jnp.broadcast_to(is_late_r, (queries, queries)), 1, 0), axis=1, keepdims=True)
+    place_r = jnp.sum(jnp.where((i0 < i1) & jnp.broadcast_to(is_late_c, (queries, queries)), 1, 0), axis=0, keepdims=True)
+    place_c = jnp.where(is_late_c, place_c, -1)
+    place_r = jnp.where(is_late_r, place_r, -1)
+
+    def one_hot(left, right):
+        return jnp.where(left == right, 1.0, 0.0).astype(bf16)
+
+    def along(n, m, axis):
+        return lax.broadcasted_iota(jnp.int32, (n, m), axis)
+
+    pick = one_hot(jnp.broadcast_to(place_r, (late_most, queries)), along(late_most, queries, 0))
+    slots_hot = one_hot(jnp.broadcast_to(slot_c, (queries, late_rows)), along(queries, late_rows, 1) + early_rows)
+    late_hot[...] = dot_nn(pick, slots_hot).astype(bf16)
+    final_c = jnp.where(is_late_c, place_c + early_rows, slot_c)
+    final_hot[...] = one_hot(jnp.broadcast_to(final_c, final_hot.shape), along(*final_hot.shape, 1))
 
     def row_pair(r):
         return pl.ds(pl.multiple_of(r * PAIR, PAIR), PAIR)
 
-    LAST = TILES - 1
+    def ready_like(n):
+        return pres.at[pl.ds(0, n), pl.ds(0, queries // 2)]
 
     def features(t):
         half = entries // 2
         return Gather(lambda h: ready.at[t, pl.ds(0, PAIR), pl.ds(h * half, half)],
                       lambda h, r: feats.at[t, row_pair(r), pl.ds(h * half, half)],
-                      lambda n: pres.at[t, pl.ds(0, n)], sems1.at[t], x, y)
-
-    last_features = Direct(ready.at[LAST, pl.ds(0, PAIR)], feats.at[LAST, row_pair(row_id)],
-                           lambda n: pres.at[LAST, pl.ds(0, n)], last1.at[SIDE], last1, x, y)
-
-    def pre_rows(t):
-        half = rows * PAIR // 2
-        return Gather(lambda h: pres.at[t, row_id, pl.ds(h * half, half)],
-                      lambda h, r: pres.at[t, r, pl.ds(h * half, half)],
-                      lambda n: pres.at[t, pl.ds(0, n)], sems2.at[t], x, y)
-
-    last_pre_rows = Direct(pres.at[LAST, row_id], pres.at[LAST, row_id],
-                           lambda n: pres.at[LAST, pl.ds(0, n)], last2.at[SIDE], last2, x, y)
+                      lambda n: ready_like(n), sems1.at[t], x, y)
+
+    def straight(t):
+        return Direct(ready.at[t, pl.ds(0, PAIR)], feats.at[t, row_pair(row_id)], ready_like, last1.at[t - RELAYED, 1],
+                      last1.at[t - RELAYED, 0], x, y)
+
+    early_half = rows * CAP // 4
+    pre_rows = Gather(lambda h: pres.at[row_id, pl.ds(h * early_half, early_half)],
+                      lambda h, r: pres.at[r, pl.ds(h * early_half, early_half)],
+                      lambda n: pres.at[pl.ds(0, n)], sems2, x, y)
+    last_pre_rows = Direct(last_pres.at[row_id], last_pres.at[row_id],
+                           lambda n: last_pres.at[pl.ds(0, n)], last2.at[SIDE], last2, x, y)
 
     def own(t):
         return pltpu.make_async_copy(ready.at[t, pl.ds(0, PAIR)], feats.at[t, row_pair(row_id)], own_sem.at[t])
@@ -214,6 +240,14 @@
         def _():
             late[0].start()
             late[1].start()
+
+        @pl.when(t == 0)
+        def _():
+            pl.semaphore_wait(barrier, rows - 1 + mods - 1)
+
+        @pl.when((t >= 2) & (t <= RELAYED + 1))
+        def _():
+            features(t - 2).forward_far()
 
         in_hi, in_lo = halves(res[0])
         in_hi = jnp.concatenate([in_hi, in_hi], axis=1)
@@ -239,80 +273,69 @@
         for r in range(rank // 2):
             ready[t, 0:PAIR, r * 128:(r + 1) * 128] = spread[r, 0:PAIR, :].astype(bf16)
 
-        @pl.when(t == 0)
-        def _():
-            pl.semaphore_wait(barrier, rows - 1 + mods - 1)
         own(t).start()
 
-        @pl.when(t != LAST)
+        @pl.when(t < RELAYED)
         def _():
             features(t).first()
 
-        @pl.when(t == LAST)
-        def _():
-            last_features.first()
-
-        @pl.when(t >= 2)
-        def _():
-            features(t - 2).forward()
+        @pl.when(t >= RELAYED)
+        def _():
+            straight(t).first()
+
+        @pl.when((t >= 1) & (t <= RELAYED))
+        def _():
+            features(t - 1).forward_near()
         return 0
     lax.fori_loop(0, TILES, token_tile, 0)
 
     late[0].wait()
 
-    def precondition(t):
-        own(t).wait()
-        chunk = 4 * share
-
+    chunk = 16 * share
+
+    def precondition(ts):
         def step(k, sums):
             at = pl.ds(pl.multiple_of(k * chunk, chunk), chunk)
-            return sums + dot_nt(feats[t, :, at], curv[:, at])
-        sums = lax.fori_loop(0, entries // chunk, step, jnp.zeros((rows * PAIR, share), f32))
-        pres[t, row_id] = sums.astype(bf16)
-
-    def batch(t, _):
-        @pl.when(t == 1)
-        def _():
-            features(2).forward()
-
-        features(t).wait()
-        precondition(t)
-        pre_rows(t).first()
-
-        @pl.when(t >= 1)
-        def _():
-            pre_rows(t - 1).forward()
-        return 0
-    lax.fori_loop(0, LAST, batch, 0)
-
-    def arrived(dx, _):
-        last_features.wait_x(dx)
-        return 0
-    lax.fori_loop(0, SIDE, arrived, 0)
-    precondition(LAST)
+            return sums + dot_nt(jnp.concatenate([feats[t, :, at] for t in ts], axis=0), curv[:, at])
+        sums = lax.fori_loop(0, entries // chunk, step, jnp.zeros((len(ts) * rows * PAIR, share), f32))
+        return sums.astype(bf16)
+
+    def turned(ts):
+        def step(k, sums):
+            at = pl.ds(pl.multiple_of(k * chunk, chunk), chunk)
+            return sums + dot_nt(curv[:, at], jnp.concatenate([feats[t, :, at] for t in ts], axis=0))
+        sums = lax.fori_loop(0, entries // chunk, step, jnp.zeros((share, len(ts) * rows * PAIR), f32))
+        return sums.astype(bf16)
+
+    for t in range(2):
+        (features(t) if t < RELAYED else straight(t)).wait()
+        own(t).wait()
+    pres[row_id] = precondition((0, 1))
+    pre_rows.first()
+    straight(2).wait()
+    own(2).wait()
+    pre_rows.forward_near()
+    pre_rows.forward_far()
+    straight(LAST).wait()
+    own(LAST).wait()
+    last_pres[row_id] = dot_nt(late_hot[...], turned((2, LAST))).astype(bf16)
     last_pre_rows.first()
-    pre_rows(LAST - 1).forward()
 
     late[1].wait()
     total[...] = jnp.zeros_like(total)
-
-    def here(t, _):
-        pre_rows(t).wait()
-        return 0
-    lax.fori_loop(0, LAST, here, 0)
+    pre_rows.wait()
 
     def source(dx, _):
         last_pre_rows.wait_x(dx)
         r = lax.rem(x + dx, SIDE) * SIDE
-        left = [jnp.concatenate([pres[t, r + k] for t in range(TILES)], axis=0) for k in range(SIDE)]
+        left = [jnp.concatenate([pres[r + k], last_pres[r + k]], axis=0) for k in range(SIDE)]
         right = store[:, pl.ds(pl.multiple_of(r * share, SIDE * share), SIDE * share)]
-        total[...] = total[...] + dot_nt(jnp.concatenate(left, axis=1), right)
+        total[...] = total[...] + dot_nt(right, jnp.concatenate(left, axis=1))
         return 0
-    lax.fori_loop(0, SIDE, source, 0)
-
-    g1 = lax.broadcasted_iota(jnp.int32, (queries, rows * CAP), 1)
-    placer = jnp.where(jnp.broadcast_to(slot_c, (queries, rows * CAP)) == g1, 1.0, 0.0).astype(bf16)
-    score[...] = dot_nn(placer, total[...].astype(bf16)).astype(bf16).reshape(score.shape)
+    for dx in range(SIDE):
+        source(dx, 0)
+
+    score[...] = dot_nt(final_hot[...], total[...].astype(bf16)).astype(bf16).reshape(score.shape)
 
     def send(d, _):
         peer = lax.rem(mod_id + d, mods)
@@ -320,19 +343,16 @@
         return 0
     lax.fori_loop(1, mods, send, 0)
     parts[mod_id] = score[mod_id]
+    for t in range(TILES):
+        (features(t) if t < RELAYED else straight(t)).finish()
+    pre_rows.finish()
+    last_pre_rows.finish()
     taken(parts.at[pl.ds(0, mods - 1)], sems3.at[1])
     summed = parts[0].astype(f32)
     for m in range(1, mods):
         summed = summed + parts[m].astype(f32)
     out_ref[...] = summed
 
-    def finish(t, _):
-        features(t).finish()
-        pre_rows(t).finish()
-        return 0
-    lax.fori_loop(0, LAST, finish, 0)
-    last_features.finish()
-    last_pre_rows.finish()
     taken(score.at[pl.ds(0, mods - 1)], sems3.at[0])
 
 
@@ -348,7 +368,7 @@
     dma = pltpu.SemaphoreType.DMA
     return pl.pallas_call(
         kernel,
-        out_shape=jax.ShapeDtypeStruct((queries // mods, held), f32),
+        out_shape=pltpu.VMEM((queries // mods, held), f32),
         in_specs=[hbm] * 8,
         out_specs=vmem,
         scratch_shapes=[
@@ -364,14 +384,17 @@
             pltpu.VMEM((rank // 2, CAP, 2 * rank), f32),
             pltpu.VMEM((TILES, CAP, rank * rank), bf16),
             pltpu.VMEM((TILES, rows * PAIR, rank * rank), bf16),
-            pltpu.VMEM((TILES, rows, rows * PAIR, share), bf16),
-            pltpu.VMEM((rows * CAP, held), f32),
+            pltpu.VMEM((rows, rows * CAP // 2, share), bf16),
+            pltpu.VMEM((rows, queries // 2, share), bf16),
+            pltpu.VMEM((queries // 2, rows * CAP // 2), bf16),
+            pltpu.VMEM((queries, rows * CAP // 2 + queries // 2), bf16),
+            pltpu.VMEM((held, rows * CAP // 2 + queries // 2), f32),
             pltpu.VMEM((mods, queries // mods, held), bf16),
             pltpu.VMEM((mods, queries // mods, held), bf16),
             (dma((2, TILES)), dma((2,)), dma((2,)), dma((2,))),
             dma((TILES,)),
-            dma((TILES - 1, 4)), dma((TILES - 1, 4)),
-            dma((SIDE + 1,)), dma((SIDE + 1,)),
+            dma((max(RELAYED,1), 4)), dma((4,)),
+            dma((TILES - RELAYED, 2)), dma((SIDE + 1,)),
             dma((2,)),
         ],
         compiler_params=pltpu.CompilerParams(collective_id=0, has_side_effects=True, vmem_limit_bytes=60 * 1024 * 1024),

time: 42.9 us -> 37.7 us (0.88)
  Pallas kernels: 41.4 us -> 37 us
  local copies, waits for them, and re-layouts: 1.35 us -> 0.61 us
    pallas_call x1, Pallas kernels: 41.4 us -> 37 us  [on_device(): pl.pallas_call(kernel, out_shape=pltpu.VMEM((queries // mods, held), f32)...]
    unnamed x1, local copies, waits for them, and re-layouts: 1.35 us -> 0.61 us
where the time goes in v3:
time: 37.7 us
  Pallas kernels  37 us (98%)
  local copies, waits for them, and re-layouts  0.61 us (2%)
    pallas_call x1, Pallas kernels, on_device(): pl.pallas_call(kernel, out_shape=pltpu.VMEM((queries // mods, held), f32)...  37 us

profile of v3, /device:TPU:1, one launch (start us, length us, event | category | flops | bytes accessed | tf_op | source)
XLA Modules:
  0.0 37.7 jit_solution(4771967379702260914)
XLA Ops:
  0.0 37.0 %shard_map.82 = f32[8,768]{1,0:T(8,128)S(1)} custom-call(s32[1,64]{1,0:T(1,128)} %bitcast.2, s32[1,64]{1,0:T(1,128)} %bitcast.3, bf16[1,1024,4096]{2,1,0:T(8,128)(2,1)} %act_h.1, bf16[1,1024,4096]{2,1,0:T(8,128)(2,1)} %grad_h.1, bf16[1,64,4096]{2,1,0:T(8,128)(2,1)} %pin_h.1, bf16[1,64,4096]{2,1,0:T(8,128)(2,1)} %pout_h.1, bf16[1,256,4096]{2,1,0:T(8,128)(2,1)} %curv_h.1, ...), custom_call_target="tpu_custom_call" | custom-call | tf_op jit(solution)/shard_map/pallas_call | solution.py:369
  37.0 0.6 %copy.10 = f32[8,768]{1,0:T(8,128)} copy(f32[8,768]{1,0:T(8,128)S(1)} %shard_map.82) | data formatting | bytes 49152

commit v4 on v3

--- a/solution.py
+++ b/solution.py
@@ -9,7 +9,7 @@
 CAP = 8
 LEN_MAX, LEN_MIN = 128, 64
 TILES = 4
-RELAYED = 1
+RELAYED = 3
 PAIR = CAP // TILES
 SIDE = 4
 FAR_FIRST = sorted(((dx, dy) for dx in range(SIDE) for dy in range(SIDE) if dx or dy),
@@ -109,9 +109,49 @@
         taken(self.blocks(SIDE * SIDE - 1), self.send)
 
 
+class Mixed:
+    def __init__(self, own, part, blocks, sems, x, y):
+        self.own, self.part, self.blocks, self.sems, self.x, self.y = own, part, blocks, sems, x, y
+
+    def at(self, dx, dy):
+        return lax.rem(self.x + dx, SIDE) * SIDE + lax.rem(self.y + dy, SIDE)
+
+    def send(self, block, place, ox, oy, dx, dy):
+        sem = SIDE if (ox, oy) == (0, 2) else SIDE + 1 if (ox, oy) == (2, 0) else ox
+        remote(block, place, self.sems.at[SIDE + 2], self.sems.at[sem], "row", self.at(dx, dy)).start()
+
+    def first(self):
+        for dx, dy in ((2, 0), (0, 2), (2, 2), (1, 1), (3, 3), (1, 3), (3, 1), (0, 1), (1, 0), (0, 3), (3, 0)):
+            self.send(self.own, self.part(self.at(0, 0)), -dx % SIDE, -dy % SIDE, dx, dy)
+
+    def forward(self):
+        for k, (ox, oy) in enumerate(((0, 2), (2, 0))):
+            taken(self.blocks(1), self.sems.at[SIDE + k])
+            block = self.part(self.at(ox, oy))
+            for d in (1, 3):
+                dx, dy = (d, 0) if ox == 0 else (0, d)
+                self.send(block, block, (ox - dx) % SIDE, (oy - dy) % SIDE, dx, dy)
+
+    def wait_x(self, dx):
+        @pl.when(dx == 0)
+        def _():
+            taken(self.blocks(2), self.sems.at[0])
+
+        @pl.when(dx == 2)
+        def _():
+            taken(self.blocks(3), self.sems.at[2])
+
+        @pl.when((dx != 0) & (dx != 2))
+        def _():
+            taken(self.blocks(4), self.sems.at[dx])
+
+    def finish(self):
+        taken(self.blocks(SIDE * SIDE - 1), self.sems.at[SIDE + 2])
+
+
 def kernel(lens_h, owners_h, act_h, grad_h, pin_h, pout_h, curv_h, store_h, out_ref,
-           lens, owners, rowsv, proj, curv, store, res, limits, acc, spread, ready, feats, pres, last_pres, late_hot, final_hot, total, score, parts,
-           in_sem, own_sem, sems1, sems2, last1, last2, sems3):
+           lens, owners, rowsv, proj, curv, store, res, limits, acc, spread, ready, feats, pres, slots_hot, total, score, parts,
+           in_sem, own_sem, sems1, sems2, last1, sems3):
     mods, rows = lax.axis_size("mod"), lax.axis_size("row")
     mod_id, row_id = lax.axis_index("mod"), lax.axis_index("row")
     x, y = row_id // SIDE, lax.rem(row_id, SIDE)
@@ -177,13 +217,6 @@
     limits[0] = jnp.broadcast_to(begin, limits.shape[1:])
     limits[1] = jnp.broadcast_to(begin + count, limits.shape[1:])
     slot_c = (rank_c // PAIR) * (rows * PAIR) + own_c * PAIR + rank_c % PAIR
-    early_rows = late_rows = rows * CAP // 2
-    late_most = queries // 2
-    is_late_r, is_late_c = rank_r >= CAP // 2, rank_c >= CAP // 2
-    place_c = jnp.sum(jnp.where((i1 < i0) & jnp.broadcast_to(is_late_r, (queries, queries)), 1, 0), axis=1, keepdims=True)
-    place_r = jnp.sum(jnp.where((i0 < i1) & jnp.broadcast_to(is_late_c, (queries, queries)), 1, 0), axis=0, keepdims=True)
-    place_c = jnp.where(is_late_c, place_c, -1)
-    place_r = jnp.where(is_late_r, place_r, -1)
 
     def one_hot(left, right):
         return jnp.where(left == right, 1.0, 0.0).astype(bf16)
@@ -191,11 +224,7 @@
     def along(n, m, axis):
         return lax.broadcasted_iota(jnp.int32, (n, m), axis)
 
-    pick = one_hot(jnp.broadcast_to(place_r, (late_most, queries)), along(late_most, queries, 0))
-    slots_hot = one_hot(jnp.broadcast_to(slot_c, (queries, late_rows)), along(queries, late_rows, 1) + early_rows)
-    late_hot[...] = dot_nn(pick, slots_hot).astype(bf16)
-    final_c = jnp.where(is_late_c, place_c + early_rows, slot_c)
-    final_hot[...] = one_hot(jnp.broadcast_to(final_c, final_hot.shape), along(*final_hot.shape, 1))
+    slots_hot[...] = one_hot(jnp.broadcast_to(slot_c, slots_hot.shape), along(*slots_hot.shape, 1))
 
     def row_pair(r):
         return pl.ds(pl.multiple_of(r * PAIR, PAIR), PAIR)
@@ -213,12 +242,7 @@
         return Direct(ready.at[t, pl.ds(0, PAIR)], feats.at[t, row_pair(row_id)], ready_like, last1.at[t - RELAYED, 1],
                       last1.at[t - RELAYED, 0], x, y)
 
-    early_half = rows * CAP // 4
-    pre_rows = Gather(lambda h: pres.at[row_id, pl.ds(h * early_half, early_half)],
-                      lambda h, r: pres.at[r, pl.ds(h * early_half, early_half)],
-                      lambda n: pres.at[pl.ds(0, n)], sems2, x, y)
-    last_pre_rows = Direct(last_pres.at[row_id], last_pres.at[row_id],
-                           lambda n: last_pres.at[pl.ds(0, n)], last2.at[SIDE], last2, x, y)
+    pre_rows = Mixed(pres.at[row_id], lambda r: pres.at[r], lambda n: pres.at[pl.ds(0, n)], sems2, x, y)
 
     def own(t):
         return pltpu.make_async_copy(ready.at[t, pl.ds(0, PAIR)], feats.at[t, row_pair(row_id)], own_sem.at[t])
@@ -245,7 +269,7 @@
         def _():
             pl.semaphore_wait(barrier, rows - 1 + mods - 1)
 
-        @pl.when((t >= 2) & (t <= RELAYED + 1))
+        @pl.when(t >= 2)
         def _():
             features(t - 2).forward_far()
 
@@ -283,70 +307,42 @@
         def _():
             straight(t).first()
 
-        @pl.when((t >= 1) & (t <= RELAYED))
+        @pl.when(t >= 1)
         def _():
             features(t - 1).forward_near()
         return 0
     lax.fori_loop(0, TILES, token_tile, 0)
 
     late[0].wait()
-
-    chunk = 16 * share
-
-    def precondition(ts):
-        def step(k, sums):
-            at = pl.ds(pl.multiple_of(k * chunk, chunk), chunk)
-            return sums + dot_nt(jnp.concatenate([feats[t, :, at] for t in ts], axis=0), curv[:, at])
-        sums = lax.fori_loop(0, entries // chunk, step, jnp.zeros((len(ts) * rows * PAIR, share), f32))
-        return sums.astype(bf16)
-
-    def turned(ts):
-        def step(k, sums):
-            at = pl.ds(pl.multiple_of(k * chunk, chunk), chunk)
-            return sums + dot_nt(curv[:, at], jnp.concatenate([feats[t, :, at] for t in ts], axis=0))
-        sums = lax.fori_loop(0, entries // chunk, step, jnp.zeros((share, len(ts) * rows * PAIR), f32))
-        return sums.astype(bf16)
-
-    for t in range(2):
+    late[1].wait()
+    features(LAST - 1).forward_far()
+    for t in range(TILES):
         (features(t) if t < RELAYED else straight(t)).wait()
         own(t).wait()
-    pres[row_id] = precondition((0, 1))
+    turned = dot_nt(curv[...], jnp.concatenate([feats[t] for t in range(TILES)], axis=0)).astype(bf16)
+    pres[row_id] = dot_nt(slots_hot[...], turned).astype(bf16)
     pre_rows.first()
-    straight(2).wait()
-    own(2).wait()
-    pre_rows.forward_near()
-    pre_rows.forward_far()
-    straight(LAST).wait()
-    own(LAST).wait()
-    last_pres[row_id] = dot_nt(late_hot[...], turned((2, LAST))).astype(bf16)
-    last_pre_rows.first()
-
-    late[1].wait()
+    pre_rows.forward()
     total[...] = jnp.zeros_like(total)
-    pre_rows.wait()
 
     def source(dx, _):
-        last_pre_rows.wait_x(dx)
+        pre_rows.wait_x(dx)
         r = lax.rem(x + dx, SIDE) * SIDE
-        left = [jnp.concatenate([pres[r + k], last_pres[r + k]], axis=0) for k in range(SIDE)]
+        left = [pres[r + k] for k in range(SIDE)]
         right = store[:, pl.ds(pl.multiple_of(r * share, SIDE * share), SIDE * share)]
         total[...] = total[...] + dot_nt(right, jnp.concatenate(left, axis=1))
         return 0
-    for dx in range(SIDE):
-        source(dx, 0)
-
-    score[...] = dot_nt(final_hot[...], total[...].astype(bf16)).astype(bf16).reshape(score.shape)
-
-    def send(d, _):
+    lax.fori_loop(0, SIDE, source, 0)
+
+    score[...] = total[...].T.astype(bf16).reshape(score.shape)
+
+    for d in (4, 5, 3, 2, 6, 7, 1):
         peer = lax.rem(mod_id + d, mods)
         remote(score.at[peer], parts.at[mod_id], sems3.at[0], sems3.at[1], "mod", peer).start()
-        return 0
-    lax.fori_loop(1, mods, send, 0)
     parts[mod_id] = score[mod_id]
     for t in range(TILES):
         (features(t) if t < RELAYED else straight(t)).finish()
     pre_rows.finish()
-    last_pre_rows.finish()
     taken(parts.at[pl.ds(0, mods - 1)], sems3.at[1])
     summed = parts[0].astype(f32)
     for m in range(1, mods):
@@ -384,17 +380,15 @@
             pltpu.VMEM((rank // 2, CAP, 2 * rank), f32),
             pltpu.VMEM((TILES, CAP, rank * rank), bf16),
             pltpu.VMEM((TILES, rows * PAIR, rank * rank), bf16),
-            pltpu.VMEM((rows, rows * CAP // 2, share), bf16),
-            pltpu.VMEM((rows, queries // 2, share), bf16),
-            pltpu.VMEM((queries // 2, rows * CAP // 2), bf16),
-            pltpu.VMEM((queries, rows * CAP // 2 + queries // 2), bf16),
-            pltpu.VMEM((held, rows * CAP // 2 + queries // 2), f32),
+            pltpu.VMEM((rows, queries, share), bf16),
+            pltpu.VMEM((queries, rows * CAP), bf16),
+            pltpu.VMEM((held, queries), f32),
             pltpu.VMEM((mods, queries // mods, held), bf16),
             pltpu.VMEM((mods, queries // mods, held), bf16),
             (dma((2, TILES)), dma((2,)), dma((2,)), dma((2,))),
             dma((TILES,)),
-            dma((max(RELAYED,1), 4)), dma((4,)),
-            dma((TILES - RELAYED, 2)), dma((SIDE + 1,)),
+            dma((max(RELAYED,1), 4)), dma((SIDE + 3,)),
+            dma((TILES - RELAYED, 2)),
             dma((2,)),
         ],
         compiler_params=pltpu.CompilerParams(collective_id=0, has_side_effects=True, vmem_limit_bytes=60 * 1024 * 1024),

time: 37.7 us -> 37 us (0.981)
  Pallas kernels: 37 us -> 36.3 us
    pallas_call x1, Pallas kernels: 37 us -> 36.3 us  [on_device(): pl.pallas_call(kernel, out_shape=pltpu.VMEM((queries // mods, held), f32)...]
where the time goes in v4:
time: 37 us; the launch traced here: 36.9 us
  Pallas kernels  36.3 us (98%)
  local copies, waits for them, and re-layouts  0.61 us (2%)
    pallas_call x1, Pallas kernels, on_device(): pl.pallas_call(kernel, out_shape=pltpu.VMEM((queries // mods, held), f32)...  36.3 us

profile of v4, /device:TPU:1, one launch (start us, length us, event | category | flops | bytes accessed | tf_op | source)
XLA Modules:
  0.0 36.9 jit_solution(17992416768001700479)
XLA Ops:
  0.0 36.3 %shard_map.82 = f32[8,768]{1,0:T(8,128)S(1)} custom-call(s32[1,64]{1,0:T(1,128)} %bitcast.2, s32[1,64]{1,0:T(1,128)} %bitcast.3, bf16[1,1024,4096]{2,1,0:T(8,128)(2,1)} %act_h.1, bf16[1,1024,4096]{2,1,0:T(8,128)(2,1)} %grad_h.1, bf16[1,64,4096]{2,1,0:T(8,128)(2,1)} %pin_h.1, bf16[1,64,4096]{2,1,0:T(8,128)(2,1)} %pout_h.1, bf16[1,256,4096]{2,1,0:T(8,128)(2,1)} %curv_h.1, ...), custom_call_target="tpu_custom_call" | custom-call | tf_op jit(solution)/shard_map/pallas_call | solution.py:365
  36.3 0.6 %copy.10 = f32[8,768]{1,0:T(8,128)} copy(f32[8,768]{1,0:T(8,128)S(1)} %shard_map.82) | data formatting | bytes 49152

commit v5 on v4

--- a/solution.py
+++ b/solution.py
@@ -313,16 +313,16 @@
         return 0
     lax.fori_loop(0, TILES, token_tile, 0)
 
-    late[0].wait()
-    late[1].wait()
     features(LAST - 1).forward_far()
     for t in range(TILES):
         (features(t) if t < RELAYED else straight(t)).wait()
         own(t).wait()
+    late[0].wait()
     turned = dot_nt(curv[...], jnp.concatenate([feats[t] for t in range(TILES)], axis=0)).astype(bf16)
     pres[row_id] = dot_nt(slots_hot[...], turned).astype(bf16)
     pre_rows.first()
     pre_rows.forward()
+    late[1].wait()
     total[...] = jnp.zeros_like(total)
 
     def source(dx, _):

time: 37 us -> 37 us (level)
  no operation moved by 1% of the time
where the time goes in v5:
time: 37 us; the launch traced here: 36.9 us
  Pallas kernels  36.3 us (98%)
  local copies, waits for them, and re-layouts  0.61 us (2%)
    pallas_call x1, Pallas kernels, on_device(): pl.pallas_call(kernel, out_shape=pltpu.VMEM((queries // mods, held), f32)...  36.3 us

profile of v5, /device:TPU:1, one launch (start us, length us, event | category | flops | bytes accessed | tf_op | source)
XLA Modules:
  0.0 36.9 jit_solution(10684769143744367987)
XLA Ops:
  0.0 36.3 %shard_map.82 = f32[8,768]{1,0:T(8,128)S(1)} custom-call(s32[1,64]{1,0:T(1,128)} %bitcast.2, s32[1,64]{1,0:T(1,128)} %bitcast.3, bf16[1,1024,4096]{2,1,0:T(8,128)(2,1)} %act_h.1, bf16[1,1024,4096]{2,1,0:T(8,128)(2,1)} %grad_h.1, bf16[1,64,4096]{2,1,0:T(8,128)(2,1)} %pin_h.1, bf16[1,64,4096]{2,1,0:T(8,128)(2,1)} %pout_h.1, bf16[1,256,4096]{2,1,0:T(8,128)(2,1)} %curv_h.1, ...), custom_call_target="tpu_custom_call" | custom-call | tf_op jit(solution)/shard_map/pallas_call | solution.py:365
  36.3 0.6 %copy.10 = f32[8,768]{1,0:T(8,128)} copy(f32[8,768]{1,0:T(8,128)S(1)} %shard_map.82) | data formatting | bytes 49152

commit v6 on v5

--- a/solution.py
+++ b/solution.py
@@ -271,6 +271,7 @@
 
         @pl.when(t >= 2)
         def _():
+            features(t - 2).forward_near()
             features(t - 2).forward_far()
 
         in_hi, in_lo = halves(res[0])
@@ -307,12 +308,10 @@
         def _():
             straight(t).first()
 
-        @pl.when(t >= 1)
-        def _():
-            features(t - 1).forward_near()
         return 0
     lax.fori_loop(0, TILES, token_tile, 0)
 
+    features(LAST - 1).forward_near()
     features(LAST - 1).forward_far()
     for t in range(TILES):
         (features(t) if t < RELAYED else straight(t)).wait()

time: 37 us -> 37 us (level)
  no operation moved by 1% of the time
where the time goes in v6:
time: 37 us; the launch traced here: 36.9 us
  Pallas kernels  36.3 us (98%)
  local copies, waits for them, and re-layouts  0.61 us (2%)
    pallas_call x1, Pallas kernels, on_device(): pl.pallas_call(kernel, out_shape=pltpu.VMEM((queries // mods, held), f32)...  36.3 us

profile of v6, /device:TPU:1, one launch (start us, length us, event | category | flops | bytes accessed | tf_op | source)
XLA Modules:
  0.0 36.9 jit_solution(5239826707269016169)
XLA Ops:
  0.0 36.3 %shard_map.82 = f32[8,768]{1,0:T(8,128)S(1)} custom-call(s32[1,64]{1,0:T(1,128)} %bitcast.2, s32[1,64]{1,0:T(1,128)} %bitcast.3, bf16[1,1024,4096]{2,1,0:T(8,128)(2,1)} %act_h.1, bf16[1,1024,4096]{2,1,0:T(8,128)(2,1)} %grad_h.1, bf16[1,64,4096]{2,1,0:T(8,128)(2,1)} %pin_h.1, bf16[1,64,4096]{2,1,0:T(8,128)(2,1)} %pout_h.1, bf16[1,256,4096]{2,1,0:T(8,128)(2,1)} %curv_h.1, ...), custom_call_target="tpu_custom_call" | custom-call | tf_op jit(solution)/shard_map/pallas_call | solution.py:364
  36.3 0.6 %copy.10 = f32[8,768]{1,0:T(8,128)} copy(f32[8,768]{1,0:T(8,128)S(1)} %shard_map.82) | data formatting | bytes 49152
